TPU v7x, 32 devices: a whole 2x2x4 slice. The times are simulated.
32 devices in a mesh: tensor: 4 (over z), dp: 4 (over y, x), seq: 2 (over core).
Axes of the slice: x: 2, y: 2, z: 4, core: 2. Of those that a mesh axis runs over, the one named last changes fastest.
Arguments:
- block_input: bfloat16 [4, 768, 1024], P('dp', 'seq'), may hold values from -6 to 6
- mixer_gain: float32 [1024], replicated, may hold values from 0.5 to 1.5
- query_weight: bfloat16 [1024, 512], P(None, 'tensor'), may hold values from -0.1875 to 0.1875
- key_weight: bfloat16 [1024, 512], P(None, 'tensor'), may hold values from -0.1875 to 0.1875
- value_weight: bfloat16 [1024, 1024], P(None, 'tensor'), may hold values from -0.1875 to 0.1875
- outgate_weight: bfloat16 [1024, 1024], P(None, 'tensor'), may hold values from -0.1875 to 0.1875
- decay_down: bfloat16 [1024, 16], replicated, may hold values from -0.1875 to 0.1875
- decay_up: bfloat16 [16, 512], P(None, 'tensor'), may hold values from -1.5 to 1.5
- decay_bias: float32 [512], P('tensor'), may hold values from -1 to 6
- group_gain: float32 [256], replicated, may hold values from 0.5 to 1.5
- output_weight: bfloat16 [1024, 1024], P('tensor'), may hold values from -0.25 to 0.25
- swiglu_gain: float32 [1024], replicated, may hold values from 0.5 to 1.5
- gate_weight: bfloat16 [1024, 2816], P(None, 'tensor'), may hold values from -0.1875 to 0.1875
- up_weight: bfloat16 [1024, 2816], P(None, 'tensor'), may hold values from -0.1875 to 0.1875
- down_weight: bfloat16 [2816, 1024], P('tensor'), may hold values from -0.15625 to 0.15625
- cotangent: bfloat16 [4, 768, 1024], P('dp', 'seq'), may hold values from -6 to 6
Outputs:
- block_output: bfloat16 [4, 768, 1024], P('dp', 'seq')
- input_gradient: float32 [4, 768, 1024], P('dp', 'seq', 'tensor')
- mixer_gradient: float32 [1024], P('tensor')
- query_gradient: float32 [1024, 512], P(('dp', 'seq'), 'tensor')
- key_gradient: float32 [1024, 512], P(('dp', 'seq'), 'tensor')
- value_gradient: float32 [1024, 1024], P(('dp', 'seq'), 'tensor')
- outgate_gradient: float32 [1024, 1024], P(('dp', 'seq'), 'tensor')
- lowrank_gradient: float32 [1024, 16], replicated
- decay_gradient: float32 [16, 512], P(None, 'tensor')
- bias_gradient: float32 [512], P('tensor')
- group_gradient: float32 [256], replicated
- output_gradient: float32 [1024, 1024], P('tensor', ('dp', 'seq'))
- swiglu_gradient: float32 [1024], replicated
- gate_gradient: float32 [1024, 2816], P(('dp', 'seq'), 'tensor')
- up_gradient: float32 [1024, 2816], P(('dp', 'seq'), 'tensor')
- down_gradient: float32 [2816, 1024], P('tensor', ('dp', 'seq'))
All inputs are finite; a program needn't handle non-finite values.
Results may differ from a plain program's by a relative error of at most 0.011.
Values sent between devices are 32-bit elements; how exact they have to be, the bound alone decides.
No kernel may reach another device: no remote copies, remote signals or barrier semaphores. Data moves between devices by JAX's collectives and lax.ppermute only.
A program may use at most 192 MiB of HBM per device.

v0:
```python
import functools

import jax
import jax.numpy as jnp
from jax import lax
from jax.experimental import pallas as pl
from jax.experimental.pallas import tpu as pltpu
from jax.sharding import PartitionSpec as P

DK = 128
DV = 256
SPAN = 64
TILE = 8
PARTS = 2
ORDER = (0, 1, 3, 2)
VMEM_LIMIT = 32 * 2**20


EPS = 1e-06
GATE_NORM = 16.0
highest_precision = lax.Precision.HIGHEST


def flip(values, axis, mask):
    count = lax.axis_size(axis)
    return lax.ppermute(values, axis, [(i, i ^ mask) for i in range(count)])


def butterfly(values, axis, first=1):
    count = lax.axis_size(axis)
    mask = first
    while mask < count:
        values = values + flip(values, axis, mask)
        mask *= 2
    return values


def after(values, *earlier):
    return lax.optimization_barrier((values, *earlier))[0]


def halves_sum(sent, kept, state):
    if lax.axis_size("tensor") == 1:
        return kept, sent
    got = flip(after(sent, *state.get("in", ())), "tensor", 1)
    state["in"] = (got,)
    kept = kept + got
    kept = butterfly(kept, "tensor", 2)
    return kept, flip(kept, "tensor", 1)


def line_gather(own):
    count = lax.axis_size("tensor")
    right = left = own
    blocks = [own]
    for step in range(1, count):
        right = lax.ppermute(right, "tensor", [(i, i + 1) for i in range(step - 1, count - 1)])
        left = lax.ppermute(left, "tensor", [(i + 1, i) for i in range(count - step)])
        blocks += [right, left]
    return blocks


def upper_half():
    return lax.axis_index("tensor") % 2


def column_block(values, block, width):
    return lax.dynamic_slice_in_dim(values, block * width, width, 1)


def direct():
    return lax.axis_size("dp") == 4 and lax.axis_size("seq") == 2


def scatter_start(sent, kept):
    size = kept[0].shape[0] // 4
    one, two = (flip(values, "seq", 1) for values in sent)
    near = slice(size, 3 * size)
    got = flip(kept[0][near] + one[near], "dp", 1)
    near = slice(2 * size, 4 * size)
    far = flip(kept[1][near] + two[near], "dp", 2)
    return kept, (one, two), (got, far)


def scatter_end(kept, sums, moved):
    size = kept[0].shape[0] // 4
    (one, two), (got, far) = sums, moved
    first, last = slice(0, size), slice(3 * size, 4 * size)
    late = flip(kept[0][last] + one[last] + got[size:], "dp", 2)
    done = kept[0][first] + one[first] + got[:size] + late
    near = slice(size, 2 * size)
    late = flip(kept[1][near] + two[near] + far[:size], "dp", 1)
    return done, kept[1][first] + two[first] + far[size:] + late


def product(left, right):
    return jnp.dot(left, right, preferred_element_type=jnp.float32)


def rms_apply(values, gain):
    return values * lax.rsqrt(jnp.mean(values * values, axis=-1, keepdims=True) + EPS) * gain


MIX_PRECISION = lax.Precision.HIGHEST


def contract(left, right, left_dim, right_dim, precision=MIX_PRECISION):
    return lax.dot_general(
        left,
        right,
        (((left_dim,), (right_dim,)), ((), ())),
        precision=precision,
        preferred_element_type=jnp.float32,
    )


def exact(left, right, left_dim, right_dim):
    return contract(left, right, left_dim, right_dim, highest_precision)


def grid_of(shape, dim):
    return lax.broadcasted_iota(jnp.int32, shape, dim)


def level_masks(span):
    row, col = grid_of((span, span), 0), grid_of((span, span), 1)
    masks = []
    half = span // 2
    while half >= TILE:
        masks.append((half, (row // (2 * half) == col // (2 * half)) & (row // half > col // half)))
        half //= 2
    return masks, (row // TILE == col // TILE) & (row >= col), col % TILE


def level_decay(cumul, half):
    rows, width = cumul.shape
    middle = [
        jnp.broadcast_to(cumul[start + half - 1 : start + half], (2 * half, width))
        for start in range(0, rows, 2 * half)
    ]
    return jnp.exp(-jnp.abs(cumul - jnp.concatenate(middle, axis=0)))


def tiles(values):
    return values.reshape(values.shape[0] // TILE, TILE, values.shape[1])


def span_scores(query, keyrow, cumul, masks, near, place):
    span = query.shape[0]
    scores = jnp.zeros((span, span), jnp.float32)
    for half, mask in masks:
        decay = level_decay(cumul, half)
        scores = scores + jnp.where(mask, contract(query * decay, keyrow * decay, 1, 1), 0.0)
    query3, key3, cumul3 = tiles(query), tiles(keyrow), tiles(cumul)
    close = jnp.zeros((span, span), jnp.float32)
    for step in range(TILE):
        decay = jnp.exp(jnp.minimum(cumul3 - cumul3[:, step : step + 1], 0.0))
        terms = (query3 * key3[:, step : step + 1] * decay).reshape(span, -1)
        close = jnp.where(place == step, jnp.sum(terms, axis=-1, keepdims=True), close)
    return scores + jnp.where(near, close, 0.0)


def triangle(span, upper):
    row, col = grid_of((span, span), 0), grid_of((span, span), 1)
    return jnp.where(row <= col if upper else row >= col, 1.0, 0.0).astype(jnp.float32)


def mix_forward(
    source_ref,
    gain_ref,
    query_w,
    key_w,
    value_w,
    outgate_w,
    down_w,
    up_w,
    bias_ref,
    normed_ref,
    query_ref,
    key_ref,
    value_ref,
    outgate_ref,
    lowrank_ref,
    logit_ref,
    cumul_ref,
    reach_ref,
    local_ref,
    state_ref,
    total_ref,
):
    length = source_ref.shape[0]
    heads = query_w.shape[1] // DK
    normed = rms_apply(source_ref[...].astype(jnp.float32), gain_ref[...]).astype(jnp.bfloat16)
    normed_ref[...] = normed
    lowrank = product(normed, down_w[...])
    lowrank_ref[...] = lowrank
    logit = exact(lowrank, up_w[...].astype(jnp.float32), 1, 0) + bias_ref[...]
    logit_ref[...] = logit
    forget = (jnp.minimum(logit, 0.0) - jnp.log1p(jnp.exp(-jnp.abs(logit)))) / GATE_NORM
    query_ref[...] = product(normed, query_w[...])
    key_ref[...] = product(normed, key_w[...])
    value_ref[...] = product(normed, value_w[...])
    outgate_ref[...] = product(normed, outgate_w[...])
    masks, near, place = level_masks(SPAN)
    lower = triangle(SPAN, False)
    scale = DK ** (-0.5)
    for head in range(heads):
        narrow = slice(head * DK, (head + 1) * DK)
        wide = slice(head * DV, (head + 1) * DV)
        state = None
        base = jnp.zeros((1, DK), jnp.float32)
        for start in range(0, length, SPAN):
            rows = slice(start, start + SPAN)
            query, keyrow, value = query_ref[rows, narrow], key_ref[rows, narrow], value_ref[rows, wide]
            cumul = exact(lower, forget[rows, narrow], 1, 0)
            cumul_ref[rows, narrow] = cumul
            last = cumul[SPAN - 1 : SPAN]
            reach_ref[rows, narrow] = query * jnp.exp(cumul + base) * scale
            base = base + last
            scores = span_scores(query, keyrow, cumul, masks, near, place)
            mixed = contract(scores, value, 1, 0)
            if state is not None:
                mixed = mixed + contract(query * jnp.exp(cumul), state, 1, 1)
            local_ref[rows, wide] = mixed * scale
            added = contract(value, keyrow * jnp.exp(last - cumul), 0, 0)
            state = added if state is None else state * jnp.exp(last) + added
        state_ref[wide, :] = state
        total_ref[head : head + 1, :] = jnp.exp(base)


def mix_backward(
    query_ref,
    key_ref,
    value_ref,
    cumul_ref,
    logit_ref,
    lowrank_ref,
    mixed_back_ref,
    state_ref,
    state_back_ref,
    up_w,
    query_back_ref,
    key_back_ref,
    value_back_ref,
    lowrank_back_ref,
    expand_ref,
    bias_ref,
    states_ref,
    logit_back_ref,
):
    length = query_ref.shape[0]
    heads = query_ref.shape[1] // DK
    count = length // SPAN
    masks, near, place = level_masks(SPAN)
    upper = triangle(SPAN, True)
    scale = DK ** (-0.5)
    final = grid_of((SPAN, DK), 0) == SPAN - 1
    lane_row = grid_of((SPAN // TILE, TILE, DK), 1)
    for head in range(heads):
        narrow = slice(head * DK, (head + 1) * DK)
        wide = slice(head * DV, (head + 1) * DV)
        state = state_ref[wide, :]
        for index in range(count):
            rows = slice(index * SPAN, (index + 1) * SPAN)
            states_ref[index] = state
            cumul = cumul_ref[rows, narrow]
            last = cumul[SPAN - 1 : SPAN]
            state = state * jnp.exp(last) + contract(
                value_ref[rows, wide], key_ref[rows, narrow] * jnp.exp(last - cumul), 0, 0
            )
        after = state
        carried = state_back_ref[wide, :]
        for index in reversed(range(count)):
            rows = slice(index * SPAN, (index + 1) * SPAN)
            query, keyrow, value = query_ref[rows, narrow], key_ref[rows, narrow], value_ref[rows, wide]
            cumul = cumul_ref[rows, narrow]
            last = cumul[SPAN - 1 : SPAN]
            back = mixed_back_ref[rows, wide] * scale
            before = states_ref[index]
            grown, rest = jnp.exp(cumul), jnp.exp(last - cumul)
            scores = span_scores(query, keyrow, cumul, masks, near, place)
            value_back = contract(scores, back, 0, 0) + contract(keyrow * rest, carried, 1, 1)
            value_back_ref[rows, wide] = value_back.astype(jnp.bfloat16)
            pairs = contract(back, value, 1, 1)
            query_back = grown * contract(back, before, 1, 0)
            key_back = rest * contract(value, carried, 1, 0)
            for half, mask in masks:
                decay = level_decay(cumul, half)
                chosen = jnp.where(mask, pairs, 0.0)
                query_back = query_back + decay * contract(chosen, keyrow * decay, 1, 0)
                key_back = key_back + decay * contract(chosen, query * decay, 0, 0)
            close = jnp.where(near, pairs, 0.0)
            query3, key3, cumul3 = tiles(query), tiles(keyrow), tiles(cumul)
            query_near = jnp.zeros_like(query3)
            key_near = jnp.zeros_like(key3)
            for step in range(TILE):
                column = jnp.sum(jnp.where(place == step, close, 0.0), axis=-1, keepdims=True)
                decay = jnp.exp(jnp.minimum(cumul3 - cumul3[:, step : step + 1], 0.0))
                weight = tiles(jnp.broadcast_to(column, (SPAN, DK))) * decay
                query_near = query_near + weight * key3[:, step : step + 1]
                total = jnp.sum(weight * query3, axis=1, keepdims=True)
                key_near = jnp.where(lane_row == step, total, key_near)
            query_back = query_back + query_near.reshape(SPAN, DK)
            key_back = key_back + key_near.reshape(SPAN, DK)
            query_back_ref[rows, narrow] = query_back.astype(jnp.bfloat16)
            key_back_ref[rows, narrow] = key_back.astype(jnp.bfloat16)
            cumul_back = query * query_back - keyrow * key_back
            ending = jnp.sum(after * carried, axis=0, keepdims=True)
            cumul_back = cumul_back + jnp.where(final, ending, 0.0)
            forget_back = exact(upper, cumul_back, 1, 0)
            logit_back_ref[rows, narrow] = forget_back * jax.nn.sigmoid(-logit_ref[rows, narrow]) / GATE_NORM
            carried = carried * jnp.exp(last) + contract(back, query * grown, 0, 0)
            after = before
    logit_back = logit_back_ref[...]
    lowrank_back_ref[...] = exact(logit_back, up_w[...].astype(jnp.float32), 1, 1).astype(jnp.bfloat16)
    expand_ref[...] = exact(lowrank_ref[...], logit_back, 0, 0)
    bias_ref[...] = jnp.sum(logit_back, axis=0, keepdims=True)


def call(kernel, outs, flops, scratch=()):
    whole = pl.BlockSpec(memory_space=pltpu.VMEM)

    def run(*args):
        moved = sum(a.size * a.dtype.itemsize for a in args)
        moved += sum(o.size * o.dtype.itemsize for o in outs)
        return pl.pallas_call(
            kernel,
            out_shape=tuple(outs),
            in_specs=[whole] * len(args),
            out_specs=tuple([whole] * len(outs)),
            scratch_shapes=list(scratch),
            compiler_params=pltpu.CompilerParams(vmem_limit_bytes=VMEM_LIMIT),
            cost_estimate=pl.CostEstimate(flops=flops, bytes_accessed=moved, transcendentals=0),
        )(*args)

    return run


def shape_of(rows, cols, kind=jnp.float32):
    return jax.ShapeDtypeStruct((rows, cols), kind)


def relay(own, total, axis, reverse):
    count = lax.axis_size(axis)
    pairs = [(i + 1, i) if reverse else (i, i + 1) for i in range(count - 1)]
    entering = None
    for _ in range(count - 1):
        sent = own if entering is None else own + total * entering
        entering = lax.ppermute(sent, axis, pairs)
    return jnp.zeros_like(own) if entering is None else entering


def split_halves(value, sent_ref, kept_ref, work_ref):
    half = value.shape[0] // 2
    work_ref[...] = value
    upper = upper_half()
    kept_ref[...] = work_ref[pl.ds(pl.multiple_of(upper * half, half), half), :]
    sent_ref[...] = work_ref[pl.ds(pl.multiple_of((1 - upper) * half, half), half), :]


def join_halves(kept_ref, other_ref, work_ref):
    half = kept_ref.shape[0]
    upper = upper_half()
    work_ref[pl.ds(pl.multiple_of(upper * half, half), half), :] = kept_ref[...]
    work_ref[pl.ds(pl.multiple_of((1 - upper) * half, half), half), :] = other_ref[...]
    return work_ref[...]


def gate_forward(local_ref, reach_ref, state_ref, outgate_ref, gain_ref, mixed_ref, gated_ref, sent_ref):
    heads = local_ref.shape[1] // DV
    for head in range(heads):
        narrow = slice(head * DK, (head + 1) * DK)
        wide = slice(head * DV, (head + 1) * DV)
        mixed = local_ref[:, wide] + contract(reach_ref[:, narrow], state_ref[wide, :], 1, 1)
        mixed_ref[:, wide] = mixed
        gate = outgate_ref[:, wide]
        gated = rms_apply(mixed, gain_ref[...]) * (gate * jax.nn.sigmoid(gate))
        gated_ref[:, wide] = gated.astype(jnp.bfloat16)
    sent_ref[...] = gated_ref[...].astype(jnp.float32)


def feed_forward(
    *refs,
    part,
):
    count = lax.axis_size("tensor")
    place = lax.axis_index("tensor")
    heads, output_w = refs[: 2 * count - 1], refs[2 * count - 1]
    size = heads[0].shape[0] // PARTS
    rows = slice(part * size, (part + 1) * size)
    span = heads[0].shape[1]
    attended = jnp.zeros((size, output_w.shape[1]), jnp.float32)
    for index, head_ref in enumerate(heads):
        step = (index + 1) // 2
        block = jnp.maximum(place - step, 0) if index % 2 else jnp.minimum(place + step, count - 1)
        weight = output_w[pl.ds(pl.multiple_of(block * span, span), span), :].astype(jnp.bfloat16)
        attended = attended + product(head_ref[rows, :].astype(jnp.bfloat16), weight)
    feed_forward_part(attended, rows, *refs[2 * count :])


def feed_forward_part(
    attended,
    rows,
    source_ref,
    upstream_ref,
    gain_ref,
    gate_w,
    up_w,
    down_w,
    middle_ref,
    second_ref,
    hidden_ref,
    back_ref,
    second_sent,
    second_kept,
    output_sent,
    output_kept,
    work_ref,
):
    units = gate_w.shape[1]
    middle = source_ref[rows, :].astype(jnp.float32) + attended
    middle_ref[...] = middle
    second = rms_apply(middle, gain_ref[...]).astype(jnp.bfloat16)
    second_ref[...] = second
    gate_pre = product(second, gate_w[...])
    up_pre = product(second, up_w[...])
    bell = jax.nn.sigmoid(gate_pre)
    silu = gate_pre * bell
    hidden = (silu * up_pre).astype(jnp.bfloat16)
    hidden_ref[...] = hidden
    hidden_back = contract(upstream_ref[rows, :], down_w[...], 1, 1, None)
    gate_back = (hidden_back * up_pre * (bell * (1.0 + gate_pre * (1.0 - bell)))).astype(jnp.bfloat16)
    up_back = (hidden_back * silu).astype(jnp.bfloat16)
    back_ref[:, :units] = gate_back
    back_ref[:, units:] = up_back
    terms = contract(gate_back, gate_w[...], 1, 1, None) + contract(up_back, up_w[...], 1, 1, None)
    split_halves(terms, second_sent, second_kept, work_ref)
    split_halves(product(hidden, down_w[...]), output_sent, output_kept, work_ref)


def join_output(*refs):
    out_ref, work_ref = refs[-2:]
    size = out_ref.shape[0] // PARTS
    for part in range(PARTS):
        kept_ref, other_ref, middle_ref = refs[3 * part : 3 * part + 3]
        total = middle_ref[...] + join_halves(kept_ref, other_ref, work_ref)
        out_ref[part * size : (part + 1) * size, :] = total.astype(jnp.bfloat16)


def gate_backward(*refs):
    parts = refs[: 3 * PARTS]
    (
        upstream_ref,
        swiglu_gain_ref,
        weight_ref,
        mixed_ref,
        outgate_ref,
        gain_ref,
        reach_ref,
        middle_round_ref,
        middle_own_ref,
        mixed_back_ref,
        outgate_back_ref,
        group_ref,
        swiglu_ref,
        self_ref,
        work_ref,
        full_ref,
    ) = refs[3 * PARTS :]
    size = work_ref.shape[0]
    swiglu = jnp.zeros_like(swiglu_ref[...])
    for part in range(PARTS):
        kept_ref, other_ref, middle_ref = parts[3 * part : 3 * part + 3]
        rows = slice(part * size, (part + 1) * size)
        second_back = join_halves(kept_ref, other_ref, work_ref)
        middle = middle_ref[...]
        root = lax.rsqrt(jnp.mean(middle * middle, axis=-1, keepdims=True) + EPS)
        unit = middle * root
        swiglu = swiglu + jnp.sum(second_back * unit, axis=0, keepdims=True)
        inner = second_back * swiglu_gain_ref[...]
        back = root * (inner - unit * jnp.mean(inner * unit, axis=-1, keepdims=True))
        back = back + upstream_ref[rows, :].astype(jnp.float32)
        full_ref[rows, :] = back
        middle_round_ref[rows, :] = back.astype(jnp.bfloat16)
    swiglu_ref[...] = swiglu
    width = middle_own_ref.shape[1]
    middle_own_ref[...] = full_ref[:, pl.ds(pl.multiple_of(lax.axis_index("tensor") * width, width), width)]
    heads = mixed_ref.shape[1] // DV
    gated_back = contract(middle_round_ref[...], weight_ref[...], 1, 1, None)
    group = jnp.zeros((1, DV), jnp.float32)
    for head in range(heads):
        narrow = slice(head * DK, (head + 1) * DK)
        wide = slice(head * DV, (head + 1) * DV)
        mixed, gate, back = mixed_ref[:, wide], outgate_ref[:, wide], gated_back[:, wide]
        root = lax.rsqrt(jnp.mean(mixed * mixed, axis=-1, keepdims=True) + EPS)
        bell = jax.nn.sigmoid(gate)
        unit = mixed * root
        outer = back * (gate * bell)
        group = group + jnp.sum(outer * unit, axis=0, keepdims=True)
        outgate_back = back * unit * gain_ref[...] * (bell * (1.0 + gate * (1.0 - bell)))
        outgate_back_ref[:, wide] = outgate_back.astype(jnp.bfloat16)
        inner = outer * gain_ref[...]
        mixed_back = root * (inner - unit * jnp.mean(inner * unit, axis=-1, keepdims=True))
        mixed_back_ref[:, wide] = mixed_back
        self_ref[wide, :] = contract(mixed_back, reach_ref[:, narrow], 0, 0)
    group_ref[...] = group


def input_terms(
    source_ref,
    gain_ref,
    normed_ref,
    query_ref,
    key_ref,
    value_ref,
    outgate_ref,
    lowrank_ref,
    query_w,
    key_w,
    value_w,
    outgate_w,
    down_w,
    group_ref,
    swiglu_ref,
    expand_ref,
    bias_ref,
    small_ref,
    inner_ref,
    own_ref,
    *rest,
):
    steps, full_ref = rest[:-1], rest[-1]
    length, width = source_ref.shape
    terms = contract(query_ref[...], query_w[...], 1, 1, None)
    terms = terms + contract(key_ref[...], key_w[...], 1, 1, None)
    terms = terms + contract(value_ref[...], value_w[...], 1, 1, None)
    terms = terms + contract(outgate_ref[...], outgate_w[...], 1, 1, None)
    terms = terms + contract(lowrank_ref[...], down_w[...], 1, 1, None)
    full_ref[...] = terms
    count = lax.axis_size("tensor")
    place = lax.axis_index("tensor")
    own = width // count

    def block(index):
        return full_ref[:, pl.ds(pl.multiple_of(index * own, own), own)]

    own_ref[...] = block(place)
    for step in range(1, count):
        steps[2 * step - 2][...] = block(jnp.minimum(count - step + place, count - 1))
        steps[2 * step - 1][...] = block(jnp.maximum(place - count + step, 0))
    source = source_ref[...].astype(jnp.float32)
    root = lax.rsqrt(jnp.mean(source * source, axis=-1, keepdims=True) + EPS)
    along = terms * source
    rank = lowrank_ref.shape[1]
    small_ref[...] = jnp.zeros_like(small_ref)
    small_ref[:rank, :] = contract(lowrank_ref[...], normed_ref[...], 0, 0, None)
    small_ref[rank : rank + 1, :] = jnp.sum(along * root, axis=0, keepdims=True)
    small_ref[rank + 1 : rank + 2, :DV] = group_ref[...]
    inner = jnp.sum(along * gain_ref[...], axis=-1, keepdims=True)
    inner_ref[...] = jnp.broadcast_to(inner, (length, 128)).T[: inner_ref.shape[0]]
    base = round_up(rank + 2, 8)
    small_ref[base : base + 1, :] = swiglu_ref[...]
    keys = bias_ref.shape[1]
    small_ref[base + 1 : base + 2, :keys] = bias_ref[...]
    many = width // keys
    for row in range(rank):
        start = row % many * keys
        line = base + 2 + row // many
        small_ref[line : line + 1, start : start + keys] = expand_ref[row : row + 1, :]


def gradient_terms(*refs):
    pairs, out_ref = refs[:-1], refs[-1]
    start = 0
    for left_ref, right_ref in zip(pairs[::2], pairs[1::2]):
        end = start + right_ref.shape[1]
        out_ref[:, start:end] = contract(left_ref[...], right_ref[...], 0, 0, None)
        start = end
    if start < out_ref.shape[1]:
        out_ref[:, start:] = jnp.zeros((out_ref.shape[0], out_ref.shape[1] - start), jnp.float32)


def round_up(count, multiple):
    return -(-count // multiple) * multiple


def gradients(pairs):
    columns = sum(right.shape[1] for _, right in pairs)
    width = pairs[0][0].shape[1]
    flat = [array for pair in pairs for array in pair]
    flops = 2 * width * columns * pairs[0][0].shape[0]
    (terms,) = call(gradient_terms, [shape_of(width, round_up(columns, 128))], flops)(*flat)
    return lax.psum_scatter(terms, ("dp", "seq"), scatter_dimension=0, tiled=True)


def gradient_blocks(*refs):
    pairs, outs = refs[:-4], refs[-4:]
    size = outs[0].shape[0] // len(ORDER)
    cut = outs[0].shape[1]
    place, own = lax.axis_index("dp"), lax.axis_index("seq")
    for far, (one_ref, two_ref) in ((1, outs[:2]), (0, outs[2:])):
        for index, step in enumerate(ORDER):
            block = (place ^ step) * 2 + (own ^ far)
            columns = pl.ds(pl.multiple_of(block * size, size), size)
            rows = slice(index * size, (index + 1) * size)
            start = 0
            for left_ref, right_ref in zip(pairs[::2], pairs[1::2]):
                count = right_ref.shape[1]
                block_sum = contract(left_ref[:, columns], right_ref[...], 0, 0, None)
                here = min(max(cut - start, 0), count)
                if here > 0:
                    one_ref[rows, start : start + here] = block_sum[:, :here]
                if here < count:
                    two_ref[rows, start + here - cut : start + count - cut] = block_sum[:, here:]
                start += count
            if start < cut + two_ref.shape[1]:
                two_ref[rows, start - cut :] = jnp.zeros((size, cut + two_ref.shape[1] - start), jnp.float32)


def gradient_start(pairs):
    columns = sum(right.shape[1] for _, right in pairs)
    width = pairs[0][0].shape[1]
    if direct():
        flat = [array for pair in pairs for array in pair]
        columns = round_up(columns, 128)
        cut = columns // 256 * 128
        halves = [shape_of(width // 2, cut), shape_of(width // 2, columns - cut)]
        flops = 2 * width * columns * pairs[0][0].shape[0]
        outs = call(gradient_blocks, halves * 2, flops)(*flat)
        return scatter_start(outs[:2], outs[2:])
    whole = jnp.concatenate([product(left.T, right) for left, right in pairs], axis=1)
    return lax.psum_scatter(whole, ("dp", "seq"), scatter_dimension=0, tiled=True)


def gradient_end(begun):
    return jnp.concatenate(scatter_end(*begun), axis=1) if direct() else begun


def on_device(
    block_input,
    mixer_gain,
    query_weight,
    key_weight,
    value_weight,
    outgate_weight,
    decay_down,
    decay_up,
    decay_bias,
    group_gain,
    output_weight,
    swiglu_gain,
    gate_weight,
    up_weight,
    down_weight,
    cotangent,
):
    rounded = jnp.bfloat16
    source, upstream = block_input[0], cotangent[0]
    length, width = source.shape
    keys, values, units = query_weight.shape[1], value_weight.shape[1], gate_weight.shape[1]
    heads = keys // DK
    rank = decay_down.shape[1]
    size = length // PARTS
    half = shape_of(size // 2, width)
    work = pltpu.VMEM((size, width), jnp.float32)
    state = {}
    share = values // (lax.axis_size("dp") * lax.axis_size("seq"))
    place = lax.axis_index("dp") * lax.axis_size("seq") + lax.axis_index("seq")
    share_rows = lax.dynamic_slice_in_dim(output_weight, place * share, share, 0).astype(jnp.float32)
    full_output_weight = lax.all_gather(share_rows, ("tensor", "dp", "seq"), axis=0, tiled=True)
    (
        normed,
        query,
        keyrow,
        value,
        outgate,
        lowrank,
        logit,
        cumul,
        reach,
        local,
        local_state,
        decay_total,
    ) = call(
        mix_forward,
        [
            shape_of(length, width, rounded),
            shape_of(length, keys),
            shape_of(length, keys),
            shape_of(length, values),
            shape_of(length, values),
            shape_of(length, rank),
            shape_of(length, keys),
            shape_of(length, keys),
            shape_of(length, keys),
            shape_of(length, values),
            shape_of(values, DK),
            shape_of(heads, DK),
        ],
        2 * length * width * (2 * keys + 2 * values),
    )(
        source,
        mixer_gain[None],
        query_weight,
        key_weight,
        value_weight,
        outgate_weight,
        decay_down,
        decay_up,
        decay_bias[None],
    )
    decay_rows = jnp.repeat(decay_total, DV, axis=0)
    incoming = relay(local_state, decay_rows, "seq", False)
    mixed, gated, sent = call(
        gate_forward,
        [shape_of(length, values), shape_of(length, values, rounded), shape_of(length, values)],
        20 * length * values,
    )(local, reach, incoming, outgate, group_gain[None])
    heads_out = line_gather(sent)
    parts = []
    for part in range(PARTS):
        parts.append(
            call(
                functools.partial(feed_forward, part=part),
                [
                    shape_of(size, width),
                    shape_of(size, width, rounded),
                    shape_of(size, units, rounded),
                    shape_of(size, 2 * units, rounded),
                    half,
                    half,
                    half,
                    half,
                ],
                12 * size * width * units,
                scratch=[work],
            )(*heads_out, full_output_weight, source, upstream, swiglu_gain[None], gate_weight, up_weight, down_weight)
        )
    second_sums = []
    for part in parts:
        second_sums += [*halves_sum(part[4], part[5], state), part[0]]
    second = jnp.concatenate([part[1] for part in parts], axis=0)
    hidden = jnp.concatenate([part[2] for part in parts], axis=0)
    units_back = jnp.concatenate([part[3] for part in parts], axis=0)
    wide_total = gradients([(second, units_back), (upstream, hidden)])
    output_sums = []
    for part in parts:
        output_sums += [*halves_sum(part[6], part[7], state), part[0]]
    (block_output,) = call(
        join_output, [shape_of(length, width, rounded)], length * width, scratch=[work]
    )(*output_sums)
    count = lax.axis_size("tensor")
    own = width // count
    middle_round, middle_own, mixed_back, outgate_round, group_part, swiglu_part, self_gradient = call(
        gate_backward,
        [
            shape_of(length, width, rounded),
            shape_of(length, own),
            shape_of(length, values),
            shape_of(length, values, rounded),
            shape_of(1, DV),
            shape_of(1, width),
            shape_of(values, DK),
        ],
        2 * length * width * values,
        scratch=[work, pltpu.VMEM((length, width), jnp.float32)],
    )(*second_sums, upstream, swiglu_gain[None], output_weight, mixed, outgate, group_gain[None], reach)
    outgoing = relay(self_gradient, decay_rows, "seq", True)
    query_round, key_round, value_round, lowrank_round, expand_part, bias_part = call(
        mix_backward,
        [
            shape_of(length, keys, rounded),
            shape_of(length, keys, rounded),
            shape_of(length, values, rounded),
            shape_of(length, rank, rounded),
            shape_of(rank, keys),
            shape_of(1, keys),
        ],
        20 * length * DK * values,
        scratch=[
            pltpu.VMEM((length // SPAN, DV, DK), jnp.float32),
            pltpu.VMEM((length, keys), jnp.float32),
        ],
    )(query, keyrow, value, cumul, logit, lowrank, mixed_back, incoming, outgoing, decay_up)
    many = width // keys
    split_rows = round_up(2 + round_up(rank, many) // many, 8)
    shared_rows = round_up(rank + 2, 8)
    small, inner, own_terms, *steps = call(
        input_terms,
        [shape_of(shared_rows + split_rows, width), shape_of(8, length)]
        + [shape_of(length, own)] * (2 * count - 1),
        2 * length * width * (2 * keys + 2 * values),
        scratch=[pltpu.VMEM((length, width), jnp.float32)],
    )(
        source,
        mixer_gain[None],
        normed,
        query_round,
        key_round,
        value_round,
        outgate_round,
        lowrank_round,
        query_weight,
        key_weight,
        value_weight,
        outgate_weight,
        decay_down,
        group_part,
        swiglu_part,
        expand_part,
        bias_part,
    )
    right = left = None
    for step in range(1, count):
        sent = steps[2 * step - 2] if right is None else steps[2 * step - 2] + right
        right = lax.ppermute(sent, "tensor", [(i, i + 1) for i in range(step)])
        sent = steps[2 * step - 1] if left is None else steps[2 * step - 1] + left
        left = lax.ppermute(sent, "tensor", [(count - 1 - i, count - 2 - i) for i in range(step)])
    mixer_begun = gradient_start(
        [
            (normed, query_round),
            (normed, key_round),
            (normed, value_round),
            (normed, outgate_round),
            (middle_round, gated),
        ],
    )
    mixer_total = gradient_end(mixer_begun)
    inner = butterfly(inner, "tensor")[0][:, None]
    small = butterfly(small, "seq")
    small = butterfly(small, "dp")
    shared = butterfly(small[:shared_rows], "tensor")
    place = lax.axis_index("tensor")
    normed_back = own_terms if right is None else own_terms + right + left
    wide_source = source.astype(jnp.float32)
    root = lax.rsqrt(jnp.mean(wide_source * wide_source, axis=-1, keepdims=True) + EPS)
    source_own = column_block(wide_source, place, own)
    weighted = normed_back * lax.dynamic_slice_in_dim(mixer_gain, place * own, own, 0)
    source_back = root * weighted - source_own * (root * root * root * inner / width)
    mixer_part = lax.dynamic_slice_in_dim(shared[rank], place * own, own, 0)
    ends = (keys, 2 * keys, 2 * keys + values, 2 * keys + 2 * values)
    expand_rows = small[shared_rows + 2 : shared_rows + 2 + round_up(rank, many) // many]
    return (
        block_output[None],
        (middle_own + source_back)[None],
        mixer_part,
        mixer_total[:, : ends[0]],
        mixer_total[:, ends[0] : ends[1]],
        mixer_total[:, ends[1] : ends[2]],
        mixer_total[:, ends[2] : ends[3]],
        shared[:rank].T,
        expand_rows.reshape(-1, keys)[:rank],
        small[shared_rows + 1, :keys],
        shared[rank + 1, :DV],
        mixer_total[:, ends[3] :].T,
        small[shared_rows],
        wide_total[:, :units],
        wide_total[:, units : 2 * units],
        wide_total[:, 2 * units : 3 * units].T,
    )


def solution(mesh):
    in_specs = (
        P("dp", "seq", None),
        P(),
        P(None, "tensor"),
        P(None, "tensor"),
        P(None, "tensor"),
        P(None, "tensor"),
        P(),
        P(None, "tensor"),
        P("tensor"),
        P(),
        P("tensor", None),
        P(),
        P(None, "tensor"),
        P(None, "tensor"),
        P("tensor", None),
        P("dp", "seq", None),
    )
    out_specs = (
        P("dp", "seq", None),
        P("dp", "seq", "tensor"),
        P("tensor"),
        P(("dp", "seq"), "tensor"),
        P(("dp", "seq"), "tensor"),
        P(("dp", "seq"), "tensor"),
        P(("dp", "seq"), "tensor"),
        P(),
        P(None, "tensor"),
        P("tensor"),
        P(),
        P("tensor", ("dp", "seq")),
        P(),
        P(("dp", "seq"), "tensor"),
        P(("dp", "seq"), "tensor"),
        P("tensor", ("dp", "seq")),
    )
    return jax.shard_map(on_device, mesh=mesh, in_specs=in_specs, out_specs=out_specs, check_vma=False)
```

profile of v0, /device:TPU:0, one launch (start us, length us, event | category | flops | bytes accessed | tf_op | source)
XLA Modules:
  0.0 314.6 jit_solution(3001793722044440644)
XLA Ops:
  16.9 5.9 %shard_map.279 = (bf16[384,1024]{1,0:T(8,128)(2,1)S(1)}, f32[384,128]{1,0:T(8,128)S(1)}, f32[384,128]{1,0:T(8,128)S(1)}, f32[384,256]{1,0:T(8,128)S(1)}, f32[384...) custom-call(bf16[384,1024]{1,0:T(8,128)(2,1)S(1)} %bitcast.22, ...), custom_call_target="tpu_custom_call" | custom-call | flops 603979776 | bytes 5506048 | tf_op jit(solution)/shard_map/pallas_call | solution.py:326
  31.0 4.3 %collective-permute-start.1 = (f32[384,256]{1,0:T(8,128)S(1)}, f32[384,256]{1,0:T(8,128)S(1)}, u32[]{:S(2)}, u32[]{:S(2)}) collective-permute-start(f32[384,256]{1,0:T(8,128)S(1)} %get-tuple-element.79.refs_0_), channel_id=1, source_target_pairs={{0,8},{8,16},{16,24},{1,9},{9,17},{17,25},{2,10},{10,18},{18,26},{... | collective-permute-start | bytes 1179656 | tf_op jit(solution)/shard_map/ppermute | solution.py:57
  37.3 11.2 %collective-permute-done.1.refs_1_ = f32[384,256]{1,0:T(8,128)S(1)} collective-permute-done((f32[384,256]{1,0:T(8,128)S(1)}, f32[384,256]{1,0:T(8,128)S(1)}, u32[]{:S(2)}, u32[]{:S(2)}) %collective-permute-start.1) | collective-permute-done | bytes 393248 | tf_op jit(solution)/shard_map/ppermute | solution.py:57
  57.4 21.1 %collective-permute-done.4.refs_4_ = f32[384,256]{1,0:T(8,128)} collective-permute-done((f32[384,256]{1,0:T(8,128)S(1)}, f32[384,256]{1,0:T(8,128)}, u32[]{:S(2)}, u32[]{:S(2)}) %collective-permute-start.4) | collective-permute-done | bytes 393248 | tf_op jit(solution)/shard_map/ppermute | solution.py:58
  84.1 4.3 %collective-permute-done.6.refs_6_ = f32[384,256]{1,0:T(8,128)} collective-permute-done((f32[384,256]{1,0:T(8,128)}, f32[384,256]{1,0:T(8,128)}, u32[]{:S(2)}, u32[]{:S(2)}) %collective-permute-start.6) | collective-permute-done | bytes 393248 | tf_op jit(solution)/shard_map/ppermute | solution.py:58
  97.6 5.2 %shard_map.282 = (f32[192,1024]{1,0:T(8,128)S(1)}, bf16[192,1024]{1,0:T(8,128)(2,1)S(1)}, bf16[192,704]{1,0:T(8,128)(2,1)S(1)}, bf16[192,1408]{1,0:T(8,128)(2,1)...) custom-call(f32[384,256]{1,0:T(8,128)S(1)} %copy-done.18, ...), custom_call_target="tpu_custom_call" | custom-call | flops 1660944384 | bytes 16412672 | tf_op jit(solution)/shard_map/pallas_call | solution.py:326
  105.8 5.5 %shard_map.281 = (f32[192,1024]{1,0:T(8,128)S(1)}, bf16[192,1024]{1,0:T(8,128)(2,1)S(1)}, bf16[192,704]{1,0:T(8,128)(2,1)S(1)}, bf16[192,1408]{1,0:T(8,128)(2,1)...) custom-call(f32[384,256]{1,0:T(8,128)S(1)} %copy-done.18, ...), custom_call_target="tpu_custom_call" | custom-call | flops 1660944384 | bytes 16412672 | tf_op jit(solution)/shard_map/pallas_call | solution.py:326
  116.5 3.5 %copy-done = f32[1024,2176]{1,0:T(8,128)} copy-done((f32[1024,2176]{1,0:T(8,128)}, f32[1024,2176]{1,0:T(8,128)S(1)}, u32[]{:S(2)}) %copy-start) | copy-done | bytes 8912920
  120.2 15.2 %collective-permute-done.7 = f32[96,1024]{1,0:T(8,128)S(1)} collective-permute-done((f32[96,1024]{1,0:T(8,128)}, f32[96,1024]{1,0:T(8,128)S(1)}, u32[]{:S(2)}, u32[]{:S(2)}) %collective-permute-start.7) | collective-permute-done | bytes 393248 | tf_op jit(solution)/shard_map/ppermute | solution.py:26
  135.5 14.9 %collective-permute-done.8 = f32[96,1024]{1,0:T(8,128)S(1)} collective-permute-done((f32[96,1024]{1,0:T(8,128)S(1)}, f32[96,1024]{1,0:T(8,128)S(1)}, u32[]{:S(2)}, u32[]{:S(2)}) %collective-permute-start.8) | collective-permute-done | bytes 393248 | tf_op jit(solution)/shard_map/ppermute | solution.py:26
  151.8 6.1 %collective-permute-done.15 = f32[96,1024]{1,0:T(8,128)S(1)} collective-permute-done((f32[96,1024]{1,0:T(8,128)S(1)}, f32[96,1024]{1,0:T(8,128)S(1)}, u32[]{:S(2)}, u32[]{:S(2)}) %collective-permute-start.15) | collective-permute-done | bytes 393248 | tf_op jit(solution)/shard_map/ppermute | solution.py:26
  158.1 6.0 %collective-permute-done.17 = f32[96,1024]{1,0:T(8,128)S(1)} collective-permute-done((f32[96,1024]{1,0:T(8,128)S(1)}, f32[96,1024]{1,0:T(8,128)S(1)}, u32[]{:S(2)}, u32[]{:S(2)}) %collective-permute-start.17) | collective-permute-done | bytes 393248 | tf_op jit(solution)/shard_map/ppermute | solution.py:26
  166.3 6.2 %collective-permute-done.16.refs_1_ = f32[96,1024]{1,0:T(8,128)S(1)} collective-permute-done((f32[96,1024]{1,0:T(8,128)S(1)}, f32[96,1024]{1,0:T(8,128)S(1)}, u32[]{:S(2)}, u32[]{:S(2)}) %collective-permute-start.16) | collective-permute-done | bytes 393248 | tf_op jit(solution)/shard_map/ppermute | solution.py:26
  172.4 7.6 %collective-permute-done.18.refs_4_ = f32[96,1024]{1,0:T(8,128)S(1)} collective-permute-done((f32[96,1024]{1,0:T(8,128)S(1)}, f32[96,1024]{1,0:T(8,128)S(1)}, u32[]{:S(2)}, u32[]{:S(2)}) %collective-permute-start.18) | collective-permute-done | bytes 393248 | tf_op jit(solution)/shard_map/ppermute | solution.py:26
  186.6 6.9 %shard_map.285 = (bf16[384,128]{1,0:T(8,128)(2,1)S(1)}, bf16[384,128]{1,0:T(8,128)(2,1)S(1)}, bf16[384,256]{1,0:T(8,128)(2,1)S(1)}, bf16[384,16]{1,0:T(8,128)(2,...) custom-call(f32[384,128]{1,0:T(8,128)S(1)} %copy-done.61, f32[384,128]{1,0:T(8,128)S(1)} %copy-done.63, ...), custom_call_target="tpu_custom_call" | custom-call | flops 251658240 | bytes 2277888 | tf_op jit(solution)/shard_map/pallas_call | solution.py:326
  203.6 9.2 %collective-permute-done.12 = f32[96,1024]{1,0:T(8,128)S(1)} collective-permute-done((f32[96,1024]{1,0:T(8,128)S(1)}, f32[96,1024]{1,0:T(8,128)S(1)}, u32[]{:S(2)}, u32[]{:S(2)}) %collective-permute-start.12) | collective-permute-done | bytes 393248 | tf_op jit(solution)/shard_map/ppermute | solution.py:26
  217.8 9.6 %collective-permute-done.10 = f32[96,1024]{1,0:T(8,128)S(1)} collective-permute-done((f32[96,1024]{1,0:T(8,128)S(1)}, f32[96,1024]{1,0:T(8,128)S(1)}, u32[]{:S(2)}, u32[]{:S(2)}) %collective-permute-start.10) | collective-permute-done | bytes 393248 | tf_op jit(solution)/shard_map/ppermute | solution.py:26
  227.5 8.1 %collective-permute-done.27 = f32[8,384]{1,0:T(8,128)S(1)} collective-permute-done((f32[8,384]{1,0:T(8,128)S(1)}, f32[8,384]{1,0:T(8,128)S(1)}, u32[]{:S(2)}, u32[]{:S(2)}) %collective-permute-start.27) | collective-permute-done | bytes 12320 | tf_op jit(solution)/shard_map/ppermute | solution.py:26
  237.9 9.5 %collective-permute-done.31 = f32[24,1024]{1,0:T(8,128)S(1)} collective-permute-done((f32[24,1024]{1,0:T(8,128)S(1)}, f32[24,1024]{1,0:T(8,128)S(1)}, u32[]{:S(2)}, u32[]{:S(2)}) %collective-permute-start.31) | collective-permute-done | bytes 98336 | tf_op jit(solution)/shard_map/ppermute | solution.py:26
  255.5 7.4 %collective-permute-start.21 = (f32[384,256]{1,0:T(8,128)S(1)}, f32[384,256]{1,0:T(8,128)S(1)}, u32[]{:S(2)}, u32[]{:S(2)}) collective-permute-start(f32[384,256]{1,0:T(8,128)S(1)} %add.141), channel_id=1, source_target_pairs={{0,8},{8,16},{1,9},{9,17},{2,10},{10,18},{3,11},{11,19},{4,12},{12... | collective-permute-start | bytes 1179656 | tf_op jit(solution)/shard_map/ppermute | solution.py:816
  270.9 4.2 %collective-permute-start.22 = (f32[384,256]{1,0:T(8,128)S(1)}, f32[384,256]{1,0:T(8,128)S(1)}, u32[]{:S(2)}, u32[]{:S(2)}) collective-permute-start(f32[384,256]{1,0:T(8,128)S(1)} %add.142), channel_id=1, source_target_pairs={{0,8},{8,16},{16,24},{1,9},{9,17},{17,25},{2,10},{10,18},{18,26},{... | collective-permute-start | bytes 1179656 | tf_op jit(solution)/shard_map/ppermute | solution.py:816
  281.8 4.4 %collective-permute-done.25 = f32[384,256]{1,0:T(8,128)S(1)} collective-permute-done((f32[384,256]{1,0:T(8,128)S(1)}, f32[384,256]{1,0:T(8,128)S(1)}, u32[]{:S(2)}, u32[]{:S(2)}) %collective-permute-start.25) | collective-permute-done | bytes 393248 | tf_op jit(solution)/shard_map/ppermute | solution.py:818
  288.1 4.3 %collective-permute-done.34 = f32[256,512]{1,0:T(8,128)S(1)} collective-permute-done((f32[256,512]{1,0:T(8,128)S(1)}, f32[256,512]{1,0:T(8,128)S(1)}, u32[]{:S(2)}, u32[]{:S(2)}) %collective-permute-start.34) | collective-permute-done | bytes 524320 | tf_op jit(solution)/shard_map/ppermute | solution.py:26
  293.4 3.5 %collective-permute-start.35 = (f32[128,512]{1,0:T(8,128)S(1)}, f32[128,512]{1,0:T(8,128)S(1)}, u32[]{:S(2)}, u32[]{:S(2)}) collective-permute-start(f32[128,512]{1,0:T(8,128)S(1)} %slice_add_fusion.6), channel_id=1, source_target_pairs={{0,4},{2,6},{4,0},{6,2},{1,5},{3,7},{5,1},{7,3},{8,12},{10,14},{12... | collective-permute-start | bytes 786440 | tf_op jit(solution)/shard_map/ppermute | solution.py:26
  (294 shorter events, 115.5 us)
Async XLA Ops:
  7.2 81.3 %all-gather.2.cloned.1.call-start = ((), (), s32[]{:S(2)}) async-start(), calls=%async_computation.1 | async-start | bytes 4325376 | tf_op jit(solution)/shard_map/all_gather | solution.py:670
  8.8 294.9 %reduce-scatter.2.cloned.1.call-start = ((), (), s32[]{:S(2)}) async-start(), calls=%async_computation.2 | async-start | bytes 10027008 | tf_op jit(solution)/shard_map/reduce_scatter | solution.py:593
  31.0 17.6 %collective-permute-start.1 = (f32[384,256]{1,0:T(8,128)S(1)}, f32[384,256]{1,0:T(8,128)S(1)}, u32[]{:S(2)}, u32[]{:S(2)}) collective-permute-start(f32[384,256]{1,0:T(8,128)S(1)} %get-tuple-element.79.refs_0_), channel_id=1, source_target_pairs={{0,8},{8,16},{16,24},{1,9},{9,17},{17,25},{2,10},{10,18},{18,26},{... | collective-permute-start | bytes 1179656 | tf_op jit(solution)/shard_map/ppermute | solution.py:57
  35.3 18.7 %collective-permute-start.2 = (f32[384,256]{1,0:T(8,128)S(1)}, f32[384,256]{1,0:T(8,128)S(1)}, u32[]{:S(2)}, u32[]{:S(2)}) collective-permute-start(f32[384,256]{1,0:T(8,128)S(1)} %get-tuple-element.79.refs_0_), channel_id=1, source_target_pairs={{8,0},{16,8},{24,16},{9,1},{17,9},{25,17},{10,2},{18,10},{26,18},{... | collective-permute-start | bytes 1179656 | tf_op jit(solution)/shard_map/ppermute | solution.py:58
  53.9 24.5 %collective-permute-start.4 = (f32[384,256]{1,0:T(8,128)S(1)}, f32[384,256]{1,0:T(8,128)}, u32[]{:S(2)}, u32[]{:S(2)}) collective-permute-start(f32[384,256]{1,0:T(8,128)S(1)} %collective-permute-done.2.refs_2_), channel_id=1, source_target_pairs={{8,0},{16,8},{9,1},{17,9},{10,2},{18,10},{11,3},{19,11},{12,4},{20... | collective-permute-start | bytes 1179656 | tf_op jit(solution)/shard_map/ppermute | solution.py:58
  56.0 28.1 %collective-permute-start.5 = (f32[384,256]{1,0:T(8,128)}, f32[384,256]{1,0:T(8,128)}, u32[]{:S(2)}, u32[]{:S(2)}) collective-permute-start(f32[384,256]{1,0:T(8,128)} %collective-permute-done.3.refs_3_), channel_id=1, source_target_pairs={{16,24},{17,25},{18,26},{19,27},{20,28},{21,29},{22,30},{23,31}} | collective-permute-start | bytes 1179656 | tf_op jit(solution)/shard_map/ppermute | solution.py:57
  120.1 15.3 %collective-permute-start.7 = (f32[96,1024]{1,0:T(8,128)}, f32[96,1024]{1,0:T(8,128)S(1)}, u32[]{:S(2)}, u32[]{:S(2)}) collective-permute-start(f32[96,1024]{1,0:T(8,128)} %copy-done.84), channel_id=1, source_target_pairs={{0,8},{8,0},{16,24},{24,16},{1,9},{9,1},{17,25},{25,17},{2,10},{10... | collective-permute-start | bytes 1179656 | tf_op jit(solution)/shard_map/ppermute | solution.py:26
  135.4 15.1 %collective-permute-start.8 = (f32[96,1024]{1,0:T(8,128)S(1)}, f32[96,1024]{1,0:T(8,128)S(1)}, u32[]{:S(2)}, u32[]{:S(2)}) collective-permute-start(f32[96,1024]{1,0:T(8,128)S(1)} %copy-done.83), channel_id=1, source_target_pairs={{0,8},{8,0},{16,24},{24,16},{1,9},{9,1},{17,25},{25,17},{2,10},{10... | collective-permute-start | bytes 1179656 | tf_op jit(solution)/shard_map/ppermute | solution.py:26
  135.5 22.5 %collective-permute-start.15 = (f32[96,1024]{1,0:T(8,128)S(1)}, f32[96,1024]{1,0:T(8,128)S(1)}, u32[]{:S(2)}, u32[]{:S(2)}) collective-permute-start(f32[96,1024]{1,0:T(8,128)S(1)} %add.135), channel_id=1, source_target_pairs={{0,16},{8,24},{16,0},{24,8},{1,17},{9,25},{17,1},{25,9},{2,18},{10... | collective-permute-start | bytes 1179656 | tf_op jit(solution)/shard_map/ppermute | solution.py:26
  164.2 15.9 %collective-permute-start.18 = (f32[96,1024]{1,0:T(8,128)S(1)}, f32[96,1024]{1,0:T(8,128)S(1)}, u32[]{:S(2)}, u32[]{:S(2)}) collective-permute-start(f32[96,1024]{1,0:T(8,128)S(1)} %add.138.refs_3_), channel_id=1, source_target_pairs={{0,8},{8,0},{16,24},{24,16},{1,9},{9,1},{17,25},{25,17},{2,10},{10... | collective-permute-start | bytes 1179656 | tf_op jit(solution)/shard_map/ppermute | solution.py:26
  164.3 32.9 %collective-permute-start.9 = (f32[96,1024]{1,0:T(8,128)S(1)}, f32[96,1024]{1,0:T(8,128)S(1)}, u32[]{:S(2)}, u32[]{:S(2)}) collective-permute-start(f32[96,1024]{1,0:T(8,128)S(1)} %copy-done.81), channel_id=1, source_target_pairs={{0,8},{8,0},{16,24},{24,16},{1,9},{9,1},{17,25},{25,17},{2,10},{10... | collective-permute-start | bytes 1179656 | tf_op jit(solution)/shard_map/ppermute | solution.py:26
  197.1 15.6 %collective-permute-start.12 = (f32[96,1024]{1,0:T(8,128)S(1)}, f32[96,1024]{1,0:T(8,128)S(1)}, u32[]{:S(2)}, u32[]{:S(2)}) collective-permute-start(f32[96,1024]{1,0:T(8,128)S(1)} %copy-done.78), channel_id=1, source_target_pairs={{0,8},{8,0},{16,24},{24,16},{1,9},{9,1},{17,25},{25,17},{2,10},{10... | collective-permute-start | bytes 1179656 | tf_op jit(solution)/shard_map/ppermute | solution.py:26
  197.2 30.1 %collective-permute-start.10 = (f32[96,1024]{1,0:T(8,128)S(1)}, f32[96,1024]{1,0:T(8,128)S(1)}, u32[]{:S(2)}, u32[]{:S(2)}) collective-permute-start(f32[96,1024]{1,0:T(8,128)S(1)} %add.131), channel_id=1, source_target_pairs={{0,16},{8,24},{16,0},{24,8},{1,17},{9,25},{17,1},{25,9},{2,18},{10... | collective-permute-start | bytes 1179656 | tf_op jit(solution)/shard_map/ppermute | solution.py:26
  200.6 62.3 %collective-permute-start.36 = (f32[512,512]{1,0:T(8,128)}, f32[512,512]{1,0:T(8,128)}, u32[]{:S(2)}, u32[]{:S(2)}) collective-permute-start(f32[512,512]{1,0:T(8,128)} %get-tuple-element.127), channel_id=1, source_target_pairs={{0,1},{1,0},{2,3},{3,2},{4,5},{5,4},{6,7},{7,6},{8,9},{9,8},{10,11... | collective-permute-start | bytes 3145736 | tf_op jit(solution)/shard_map/ppermute | solution.py:26
  200.8 14.6 %collective-permute-start.26 = (f32[8,384]{1,0:T(8,128)S(1)}, f32[8,384]{1,0:T(8,128)S(1)}, u32[]{:S(2)}, u32[]{:S(2)}) collective-permute-start(f32[8,384]{1,0:T(8,128)S(1)} %get-tuple-element.120), channel_id=1, source_target_pairs={{0,8},{8,0},{16,24},{24,16},{1,9},{9,1},{17,25},{25,17},{2,10},{10... | collective-permute-start | bytes 36872 | tf_op jit(solution)/shard_map/ppermute | solution.py:26
  212.8 24.9 %collective-permute-start.13 = (f32[96,1024]{1,0:T(8,128)S(1)}, f32[96,1024]{1,0:T(8,128)S(1)}, u32[]{:S(2)}, u32[]{:S(2)}) collective-permute-start(f32[96,1024]{1,0:T(8,128)S(1)} %add.133), channel_id=1, source_target_pairs={{0,16},{8,24},{16,0},{24,8},{1,17},{9,25},{17,1},{25,9},{2,18},{10... | collective-permute-start | bytes 1179656 | tf_op jit(solution)/shard_map/ppermute | solution.py:26
  215.4 20.1 %collective-permute-start.27 = (f32[8,384]{1,0:T(8,128)S(1)}, f32[8,384]{1,0:T(8,128)S(1)}, u32[]{:S(2)}, u32[]{:S(2)}) collective-permute-start(f32[8,384]{1,0:T(8,128)S(1)} %add.148), channel_id=1, source_target_pairs={{0,16},{8,24},{16,0},{24,8},{1,17},{9,25},{17,1},{25,9},{2,18},{10... | collective-permute-start | bytes 36872 | tf_op jit(solution)/shard_map/ppermute | solution.py:26
  215.9 21.7 %collective-permute-start.30 = (f32[32,1024]{1,0:T(8,128)S(1)}, f32[32,1024]{1,0:T(8,128)S(1)}, u32[]{:S(2)}, u32[]{:S(2)}) collective-permute-start(f32[32,1024]{1,0:T(8,128)S(1)} %add.152), channel_id=1, source_target_pairs={{0,4},{2,6},{4,0},{6,2},{1,5},{3,7},{5,1},{7,3},{8,12},{10,14},{12... | collective-permute-start | bytes 393224 | tf_op jit(solution)/shard_map/ppermute | solution.py:26
  227.4 37.4 %collective-permute-start.11 = (f32[96,1024]{1,0:T(8,128)S(1)}, f32[96,1024]{1,0:T(8,128)}, u32[]{:S(2)}, u32[]{:S(2)}) collective-permute-start(f32[96,1024]{1,0:T(8,128)S(1)} %add.132.refs_0_), channel_id=1, source_target_pairs={{0,8},{8,0},{16,24},{24,16},{1,9},{9,1},{17,25},{25,17},{2,10},{10... | collective-permute-start | bytes 1179656 | tf_op jit(solution)/shard_map/ppermute | solution.py:26
  237.7 38.8 %collective-permute-start.33 = (f32[512,512]{1,0:T(8,128)}, f32[512,512]{1,0:T(8,128)}, u32[]{:S(2)}, u32[]{:S(2)}) collective-permute-start(f32[512,512]{1,0:T(8,128)} %get-tuple-element.125), channel_id=1, source_target_pairs={{0,1},{1,0},{2,3},{3,2},{4,5},{5,4},{6,7},{7,6},{8,9},{9,8},{10,11... | collective-permute-start | bytes 3145736 | tf_op jit(solution)/shard_map/ppermute | solution.py:26
  251.8 16.8 %collective-permute-start.14 = (f32[96,1024]{1,0:T(8,128)S(1)}, f32[96,1024]{1,0:T(8,128)S(1)}, u32[]{:S(2)}, u32[]{:S(2)}) collective-permute-start(f32[96,1024]{1,0:T(8,128)S(1)} %add.134.refs_3_), channel_id=1, source_target_pairs={{0,8},{8,0},{16,24},{24,16},{1,9},{9,1},{17,25},{25,17},{2,10},{10... | collective-permute-start | bytes 1179656 | tf_op jit(solution)/shard_map/ppermute | solution.py:26
  255.5 15.3 %collective-permute-start.21 = (f32[384,256]{1,0:T(8,128)S(1)}, f32[384,256]{1,0:T(8,128)S(1)}, u32[]{:S(2)}, u32[]{:S(2)}) collective-permute-start(f32[384,256]{1,0:T(8,128)S(1)} %add.141), channel_id=1, source_target_pairs={{0,8},{8,16},{1,9},{9,17},{2,10},{10,18},{3,11},{11,19},{4,12},{12... | collective-permute-start | bytes 1179656 | tf_op jit(solution)/shard_map/ppermute | solution.py:816
  277.7 14.7 %collective-permute-start.34 = (f32[256,512]{1,0:T(8,128)S(1)}, f32[256,512]{1,0:T(8,128)S(1)}, u32[]{:S(2)}, u32[]{:S(2)}) collective-permute-start(f32[256,512]{1,0:T(8,128)S(1)} %slice_add_fusion.1), channel_id=1, source_target_pairs={{0,2},{2,0},{4,6},{6,4},{1,3},{3,1},{5,7},{7,5},{8,10},{10,8},{12,... | collective-permute-start | bytes 1572872 | tf_op jit(solution)/shard_map/ppermute | solution.py:26
  278.8 18.1 %collective-permute-start.38 = (f32[128,512]{1,0:T(8,128)S(1)}, f32[128,512]{1,0:T(8,128)S(1)}, u32[]{:S(2)}, u32[]{:S(2)}) collective-permute-start(f32[128,512]{1,0:T(8,128)S(1)} %slice_add_fusion.2), channel_id=1, source_target_pairs={{0,2},{2,0},{4,6},{6,4},{1,3},{3,1},{5,7},{7,5},{8,10},{10,8},{12,... | collective-permute-start | bytes 786440 | tf_op jit(solution)/shard_map/ppermute | solution.py:26
  (102 other events, 917.5 us)
Sparse Core Ops, SparseCore 0:
  11.4 67.9 all-gather.1
  120.2 71.8 reduce-scatter.1
where the time goes:
time: 317 us; the launch traced here: 315 us
  waiting for transfers between devices  149 us (47%)
  starting transfers between devices  49.6 us (16%)
  local copies, waits for them, and re-layouts  49.6 us (16%)
  Pallas kernels  36.3 us (11%)
  other arithmetic  15.6 us (5%)
  between operations  15 us (5%)
    ppermute x25, waiting for transfers between devices, flip(): return lax.ppermute(values, axis, [(i, i ^ mask) for i in range(count)])  101 us
    unnamed x177, local copies, waits for them, and re-layouts  42.6 us
    pallas_call x10, Pallas kernels, run(): pl.pallas_call(kernel, out_shape=tuple(outs), in_specs=[whole] * len(args...  36.3 us
    ppermute x3, waiting for transfers between devices, line_gather(): lax.ppermute(left, 'tensor', [(i + 1, i) for i in range(count - step)])  28.7 us
    ppermute x25, starting transfers between devices, flip(): return lax.ppermute(values, axis, [(i, i ^ mask) for i in range(count)])  17.3 us
    ppermute x3, starting transfers between devices, on_device(): right = lax.ppermute(sent, 'tensor', [(i, i + 1) for i in range(step)])  13.6 us
    ppermute x3, waiting for transfers between devices, line_gather(): lax.ppermute(right, 'tensor', [(i, i + 1) for i in range(step - 1, count...  11.2 us
    ppermute x3, starting transfers between devices, line_gather(): lax.ppermute(right, 'tensor', [(i, i + 1) for i in range(step - 1, count...  7.13 us
  transfers between devices with their start and end apart: 41, of which 21 were waited for; matrix products, arithmetic and copies ran while one was open for 8% of the time, Pallas kernels for 7%

commit v1 on v0

--- a/solution.py
+++ b/solution.py
@@ -192,7 +192,7 @@
     heads = query_w.shape[1] // DK
     normed = rms_apply(source_ref[...].astype(jnp.float32), gain_ref[...]).astype(jnp.bfloat16)
     normed_ref[...] = normed
-    lowrank = product(normed, down_w[...])
+    lowrank = contract(normed, down_w[...], 1, 1, None)
     lowrank_ref[...] = lowrank
     logit = exact(lowrank, up_w[...].astype(jnp.float32), 1, 0) + bias_ref[...]
     logit_ref[...] = logit
@@ -417,13 +417,13 @@
     output_kept,
     work_ref,
 ):
-    units = gate_w.shape[1]
+    units = gate_w.shape[0]
     middle = source_ref[rows, :].astype(jnp.float32) + attended
     middle_ref[...] = middle
     second = rms_apply(middle, gain_ref[...]).astype(jnp.bfloat16)
     second_ref[...] = second
-    gate_pre = product(second, gate_w[...])
-    up_pre = product(second, up_w[...])
+    gate_pre = contract(second, gate_w[...], 1, 1, None)
+    up_pre = contract(second, up_w[...], 1, 1, None)
     bell = jax.nn.sigmoid(gate_pre)
     silu = gate_pre * bell
     hidden = (silu * up_pre).astype(jnp.bfloat16)
@@ -433,7 +433,7 @@
     up_back = (hidden_back * silu).astype(jnp.bfloat16)
     back_ref[:, :units] = gate_back
     back_ref[:, units:] = up_back
-    terms = contract(gate_back, gate_w[...], 1, 1, None) + contract(up_back, up_w[...], 1, 1, None)
+    terms = product(gate_back, gate_w[...]) + product(up_back, up_w[...])
     split_halves(terms, second_sent, second_kept, work_ref)
     split_halves(product(hidden, down_w[...]), output_sent, output_kept, work_ref)
 
@@ -525,17 +525,15 @@
     expand_ref,
     bias_ref,
     small_ref,
-    inner_ref,
-    own_ref,
     *rest,
 ):
-    steps, full_ref = rest[:-1], rest[-1]
+    blocks, full_ref = rest[:-1], rest[-1]
     length, width = source_ref.shape
     terms = contract(query_ref[...], query_w[...], 1, 1, None)
     terms = terms + contract(key_ref[...], key_w[...], 1, 1, None)
     terms = terms + contract(value_ref[...], value_w[...], 1, 1, None)
     terms = terms + contract(outgate_ref[...], outgate_w[...], 1, 1, None)
-    terms = terms + contract(lowrank_ref[...], down_w[...], 1, 1, None)
+    terms = terms + product(lowrank_ref[...], down_w[...])
     full_ref[...] = terms
     count = lax.axis_size("tensor")
     place = lax.axis_index("tensor")
@@ -544,10 +542,10 @@
     def block(index):
         return full_ref[:, pl.ds(pl.multiple_of(index * own, own), own)]
 
-    own_ref[...] = block(place)
+    blocks[0][:length, :] = block(place)
     for step in range(1, count):
-        steps[2 * step - 2][...] = block(jnp.minimum(count - step + place, count - 1))
-        steps[2 * step - 1][...] = block(jnp.maximum(place - count + step, 0))
+        blocks[2 * step - 1][:length, :] = block(jnp.minimum(count - step + place, count - 1))
+        blocks[2 * step][:length, :] = block(jnp.maximum(place - count + step, 0))
     source = source_ref[...].astype(jnp.float32)
     root = lax.rsqrt(jnp.mean(source * source, axis=-1, keepdims=True) + EPS)
     along = terms * source
@@ -557,7 +555,12 @@
     small_ref[rank : rank + 1, :] = jnp.sum(along * root, axis=0, keepdims=True)
     small_ref[rank + 1 : rank + 2, :DV] = group_ref[...]
     inner = jnp.sum(along * gain_ref[...], axis=-1, keepdims=True)
-    inner_ref[...] = jnp.broadcast_to(inner, (length, 128)).T[: inner_ref.shape[0]]
+    inner = jnp.broadcast_to(inner, (length, 128)).T[:1]
+    for block_ref in blocks:
+        block_ref[length:, :] = jnp.zeros((block_ref.shape[0] - length, own), jnp.float32)
+        for line, start in enumerate(range(0, length, own)):
+            end = min(start + own, length)
+            block_ref[length + line : length + line + 1, : end - start] = inner[:, start:end]
     base = round_up(rank + 2, 8)
     small_ref[base : base + 1, :] = swiglu_ref[...]
     keys = bias_ref.shape[1]
@@ -705,7 +708,7 @@
         key_weight,
         value_weight,
         outgate_weight,
-        decay_down,
+        decay_down.T,
         decay_up,
         decay_bias[None],
     )
@@ -734,7 +737,7 @@
                 ],
                 12 * size * width * units,
                 scratch=[work],
-            )(*heads_out, full_output_weight, source, upstream, swiglu_gain[None], gate_weight, up_weight, down_weight)
+            )(*heads_out, full_output_weight, source, upstream, swiglu_gain[None], gate_weight.T, up_weight.T, down_weight)
         )
     second_sums = []
     for part in parts:
@@ -785,10 +788,11 @@
     many = width // keys
     split_rows = round_up(2 + round_up(rank, many) // many, 8)
     shared_rows = round_up(rank + 2, 8)
-    small, inner, own_terms, *steps = call(
+    lines = -(-length // own)
+    small, own_terms, *steps = call(
         input_terms,
-        [shape_of(shared_rows + split_rows, width), shape_of(8, length)]
-        + [shape_of(length, own)] * (2 * count - 1),
+        [shape_of(shared_rows + split_rows, width)]
+        + [shape_of(length + round_up(lines, 8), own)] * (2 * count - 1),
         2 * length * width * (2 * keys + 2 * values),
         scratch=[pltpu.VMEM((length, width), jnp.float32)],
     )(
@@ -804,7 +808,7 @@
         key_weight,
         value_weight,
         outgate_weight,
-        decay_down,
+        decay_down.T,
         group_part,
         swiglu_part,
         expand_part,
@@ -826,12 +830,16 @@
         ],
     )
     mixer_total = gradient_end(mixer_begun)
-    inner = butterfly(inner, "tensor")[0][:, None]
     small = butterfly(small, "seq")
     small = butterfly(small, "dp")
-    shared = butterfly(small[:shared_rows], "tensor")
+    shared, mask = small[:shared_rows], 1
+    while mask < count:
+        shared = shared + flip(shared, "tensor", mask)
+        mask *= 2
     place = lax.axis_index("tensor")
-    normed_back = own_terms if right is None else own_terms + right + left
+    total = own_terms if right is None else own_terms + right + left
+    normed_back = total[:length]
+    inner = total[length : length + lines].reshape(-1, 1)[:length]
     wide_source = source.astype(jnp.float32)
     root = lax.rsqrt(jnp.mean(wide_source * wide_source, axis=-1, keepdims=True) + EPS)
     source_own = column_block(wide_source, place, own)

time: 317 us -> 308 us (0.972)
  waiting for transfers between devices: 149 us -> 130 us
  starting transfers between devices: 49.6 us -> 57 us
  other arithmetic: 15.6 us -> 19.1 us
    ppermute x25 -> x23, waiting for transfers between devices: 101 us -> 81.1 us  [flip(): return lax.ppermute(values, axis, [(i, i ^ mask) for i in range(count)])]
    ppermute x25 -> x23, starting transfers between devices: 17.3 us -> 28.1 us  [flip(): return lax.ppermute(values, axis, [(i, i ^ mask) for i in range(count)])]
    ppermute x3, waiting for transfers between devices: 4.37 us -> 0.01 us  [on_device(): lax.ppermute(sent, 'tensor', [(count - 1 - i, count - 2 - i) for i in ran...]
    unnamed x177 -> x186, local copies, waits for them, and re-layouts: 42.6 us -> 42.3 us
  transfers between devices with their start and end apart: 41 -> 39, of which waited for: 21 -> 23; matrix products, arithmetic and copies ran while one was open for 8% -> 8% of each run, Pallas kernels for 7% -> 8%
where the time goes in v1:
time: 308 us; the launch traced here: 304 us
  waiting for transfers between devices  130 us (42%)
  starting transfers between devices  57 us (19%)
  local copies, waits for them, and re-layouts  49.3 us (16%)
  Pallas kernels  33.7 us (11%)
  other arithmetic  19.1 us (6%)
  between operations  14.9 us (5%)
    ppermute x23, waiting for transfers between devices, flip(): return lax.ppermute(values, axis, [(i, i ^ mask) for i in range(count)])  81.1 us
    unnamed x186, local copies, waits for them, and re-layouts  42.3 us
    pallas_call x10, Pallas kernels, run(): pl.pallas_call(kernel, out_shape=tuple(outs), in_specs=[whole] * len(args...  33.7 us
    ppermute x3, waiting for transfers between devices, line_gather(): lax.ppermute(left, 'tensor', [(i + 1, i) for i in range(count - step)])  31.1 us
    ppermute x23, starting transfers between devices, flip(): return lax.ppermute(values, axis, [(i, i ^ mask) for i in range(count)])  28.1 us
    ppermute x3, waiting for transfers between devices, line_gather(): lax.ppermute(right, 'tensor', [(i, i + 1) for i in range(step - 1, count...  12.2 us
    ppermute x3, starting transfers between devices, on_device(): right = lax.ppermute(sent, 'tensor', [(i, i + 1) for i in range(step)])  11.6 us
  transfers between devices with their start and end apart: 39, of which 23 were waited for; matrix products, arithmetic and copies ran while one was open for 8% of the time, Pallas kernels for 8%

profile of v1, /device:TPU:0, one launch (start us, length us, event | category | flops | bytes accessed | tf_op | source)
XLA Modules:
  0.0 304.5 jit_solution(15292607514696194629)
XLA Ops:
  16.7 5.9 %shard_map.279 = (bf16[384,1024]{1,0:T(8,128)(2,1)S(1)}, f32[384,128]{1,0:T(8,128)S(1)}, f32[384,128]{1,0:T(8,128)S(1)}, f32[384,256]{1,0:T(8,128)S(1)}, f32[384...) custom-call(bf16[384,1024]{1,0:T(8,128)(2,1)S(1)} %bitcast.30, ...), custom_call_target="tpu_custom_call" | custom-call | flops 603979776 | bytes 5506048 | tf_op jit(solution)/shard_map/pallas_call | solution.py:326
  31.5 4.3 %collective-permute-start.1 = (f32[384,256]{1,0:T(8,128)S(1)}, f32[384,256]{1,0:T(8,128)S(1)}, u32[]{:S(2)}, u32[]{:S(2)}) collective-permute-start(f32[384,256]{1,0:T(8,128)S(1)} %get-tuple-element.78.refs_0_), channel_id=1, source_target_pairs={{0,8},{8,16},{16,24},{1,9},{9,17},{17,25},{2,10},{10,18},{18,26},{... | collective-permute-start | bytes 1179656 | tf_op jit(solution)/shard_map/ppermute | solution.py:57
  37.1 12.2 %collective-permute-done.1.refs_1_ = f32[384,256]{1,0:T(8,128)S(1)} collective-permute-done((f32[384,256]{1,0:T(8,128)S(1)}, f32[384,256]{1,0:T(8,128)S(1)}, u32[]{:S(2)}, u32[]{:S(2)}) %collective-permute-start.1) | collective-permute-done | bytes 393248 | tf_op jit(solution)/shard_map/ppermute | solution.py:57
  50.7 3.7 %collective-permute-done.2.refs_2_ = f32[384,256]{1,0:T(8,128)S(1)} collective-permute-done((f32[384,256]{1,0:T(8,128)S(1)}, f32[384,256]{1,0:T(8,128)S(1)}, u32[]{:S(2)}, u32[]{:S(2)}) %collective-permute-start.2) | collective-permute-done | bytes 393248 | tf_op jit(solution)/shard_map/ppermute | solution.py:58
  57.9 20.7 %collective-permute-done.4.refs_4_ = f32[384,256]{1,0:T(8,128)S(1)} collective-permute-done((f32[384,256]{1,0:T(8,128)S(1)}, f32[384,256]{1,0:T(8,128)S(1)}, u32[]{:S(2)}, u32[]{:S(2)}) %collective-permute-start.4) | collective-permute-done | bytes 393248 | tf_op jit(solution)/shard_map/ppermute | solution.py:58
  81.6 6.7 %collective-permute-done.6.refs_6_ = f32[384,256]{1,0:T(8,128)S(1)} collective-permute-done((f32[384,256]{1,0:T(8,128)S(1)}, f32[384,256]{1,0:T(8,128)S(1)}, u32[]{:S(2)}, u32[]{:S(2)}) %collective-permute-start.6) | collective-permute-done | bytes 393248 | tf_op jit(solution)/shard_map/ppermute | solution.py:58
  101.2 3.9 %shard_map.281 = (f32[192,1024]{1,0:T(8,128)S(1)}, bf16[192,1024]{1,0:T(8,128)(2,1)S(1)}, bf16[192,704]{1,0:T(8,128)(2,1)S(1)}, bf16[192,1408]{1,0:T(8,128)(2,1)...) custom-call(f32[384,256]{1,0:T(8,128)S(1)} %get-tuple-element.78.refs_0, ...), custom_call_target="tpu_custom_call" | custom-call | flops 1660944384 | bytes 16412672 | tf_op jit(solution)/shard_map/pallas_call | solution.py:326
  108.1 3.9 %shard_map.282 = (f32[192,1024]{1,0:T(8,128)S(1)}, bf16[192,1024]{1,0:T(8,128)(2,1)S(1)}, bf16[192,704]{1,0:T(8,128)(2,1)S(1)}, bf16[192,1408]{1,0:T(8,128)(2,1)...) custom-call(f32[384,256]{1,0:T(8,128)S(1)} %get-tuple-element.78.refs_0, ...), custom_call_target="tpu_custom_call" | custom-call | flops 1660944384 | bytes 16412672 | tf_op jit(solution)/shard_map/pallas_call | solution.py:326
  116.0 3.6 %copy-done = f32[1024,2176]{1,0:T(8,128)} copy-done((f32[1024,2176]{1,0:T(8,128)}, f32[1024,2176]{1,0:T(8,128)S(1)}, u32[]{:S(2)}) %copy-start) | copy-done | bytes 8912920
  119.7 16.0 %collective-permute-done.7 = f32[96,1024]{1,0:T(8,128)S(1)} collective-permute-done((f32[96,1024]{1,0:T(8,128)}, f32[96,1024]{1,0:T(8,128)S(1)}, u32[]{:S(2)}, u32[]{:S(2)}) %collective-permute-start.7) | collective-permute-done | bytes 393248 | tf_op jit(solution)/shard_map/ppermute | solution.py:26
  137.9 16.2 %collective-permute-done.8 = f32[96,1024]{1,0:T(8,128)S(1)} collective-permute-done((f32[96,1024]{1,0:T(8,128)}, f32[96,1024]{1,0:T(8,128)S(1)}, u32[]{:S(2)}, u32[]{:S(2)}) %collective-permute-start.8) | collective-permute-done | bytes 393248 | tf_op jit(solution)/shard_map/ppermute | solution.py:26
  157.1 9.7 %collective-permute-done.17 = f32[96,1024]{1,0:T(8,128)S(1)} collective-permute-done((f32[96,1024]{1,0:T(8,128)S(1)}, f32[96,1024]{1,0:T(8,128)S(1)}, u32[]{:S(2)}, u32[]{:S(2)}) %collective-permute-start.17) | collective-permute-done | bytes 393248 | tf_op jit(solution)/shard_map/ppermute | solution.py:26
  171.5 6.2 %collective-permute-done.18.refs_4_ = f32[96,1024]{1,0:T(8,128)S(1)} collective-permute-done((f32[96,1024]{1,0:T(8,128)S(1)}, f32[96,1024]{1,0:T(8,128)S(1)}, u32[]{:S(2)}, u32[]{:S(2)}) %collective-permute-start.18) | collective-permute-done | bytes 393248 | tf_op jit(solution)/shard_map/ppermute | solution.py:26
  184.5 6.9 %shard_map.285 = (bf16[384,128]{1,0:T(8,128)(2,1)S(1)}, bf16[384,128]{1,0:T(8,128)(2,1)S(1)}, bf16[384,256]{1,0:T(8,128)(2,1)S(1)}, bf16[384,16]{1,0:T(8,128)(2,...) custom-call(f32[384,128]{1,0:T(8,128)S(1)} %copy-done.65, f32[384,128]{1,0:T(8,128)S(1)} %copy-done.67, ...), custom_call_target="tpu_custom_call" | custom-call | flops 251658240 | bytes 2277888 | tf_op jit(solution)/shard_map/pallas_call | solution.py:326
  191.6 2.8 shard_map.286
  198.0 3.3 %collective-permute-done.27 = f32[32,1024]{1,0:T(8,128)S(1)} collective-permute-done((f32[32,1024]{1,0:T(8,128)S(1)}, f32[32,1024]{1,0:T(8,128)S(1)}, u32[]{:S(2)}, u32[]{:S(2)}) %collective-permute-start.27) | collective-permute-done | bytes 131104 | tf_op jit(solution)/shard_map/ppermute | solution.py:26
  204.6 9.3 %collective-permute-done.12 = f32[96,1024]{1,0:T(8,128)S(1)} collective-permute-done((f32[96,1024]{1,0:T(8,128)S(1)}, f32[96,1024]{1,0:T(8,128)S(1)}, u32[]{:S(2)}, u32[]{:S(2)}) %collective-permute-start.12) | collective-permute-done | bytes 393248 | tf_op jit(solution)/shard_map/ppermute | solution.py:26
  215.2 2.6 shard_map.287
  220.7 6.5 %collective-permute-done.10 = f32[96,1024]{1,0:T(8,128)S(1)} collective-permute-done((f32[96,1024]{1,0:T(8,128)S(1)}, f32[96,1024]{1,0:T(8,128)S(1)}, u32[]{:S(2)}, u32[]{:S(2)}) %collective-permute-start.10) | collective-permute-done | bytes 393248 | tf_op jit(solution)/shard_map/ppermute | solution.py:26
  227.3 4.7 %collective-permute-start.20 = (f32[392,256]{1,0:T(8,128)}, f32[392,256]{1,0:T(8,128)}, u32[]{:S(2)}, u32[]{:S(2)}) collective-permute-start(f32[392,256]{1,0:T(8,128)} %get-tuple-element.115), channel_id=1, source_target_pairs={{0,8},{1,9},{2,10},{3,11},{4,12},{5,13},{6,14},{7,15}} | collective-permute-start | bytes 1204232 | tf_op jit(solution)/shard_map/ppermute | solution.py:820
  235.3 4.7 %collective-permute-start.30 = (f32[24,1024]{1,0:T(8,128)S(1)}, f32[24,1024]{1,0:T(8,128)S(1)}, u32[]{:S(2)}, u32[]{:S(2)}) collective-permute-start(f32[24,1024]{1,0:T(8,128)S(1)} %slice_add_fusion.10), channel_id=1, source_target_pairs={{0,16},{8,24},{16,0},{24,8},{1,17},{9,25},{17,1},{25,9},{2,18},{10... | collective-permute-start | bytes 294920 | tf_op jit(solution)/shard_map/ppermute | solution.py:26
  262.2 4.4 %collective-permute-start.22 = (f32[392,256]{1,0:T(8,128)S(1)}, f32[392,256]{1,0:T(8,128)S(1)}, u32[]{:S(2)}, u32[]{:S(2)}) collective-permute-start(f32[392,256]{1,0:T(8,128)S(1)} %add.140), channel_id=1, source_target_pairs={{0,8},{8,16},{16,24},{1,9},{9,17},{17,25},{2,10},{10,18},{18,26},{... | collective-permute-start | bytes 1204232 | tf_op jit(solution)/shard_map/ppermute | solution.py:820
  272.7 6.0 %collective-permute-done.32 = f32[256,512]{1,0:T(8,128)S(1)} collective-permute-done((f32[256,512]{1,0:T(8,128)S(1)}, f32[256,512]{1,0:T(8,128)S(1)}, u32[]{:S(2)}, u32[]{:S(2)}) %collective-permute-start.32) | collective-permute-done | bytes 524320 | tf_op jit(solution)/shard_map/ppermute | solution.py:26
  283.3 2.7 collective-permute-start.36
  (299 shorter events, 122.8 us)
Async XLA Ops:
  7.2 81.8 %all-gather.2.cloned.1.call-start = ((), (), s32[]{:S(2)}) async-start(), calls=%async_computation.1 | async-start | bytes 4325376 | tf_op jit(solution)/shard_map/all_gather | solution.py:673
  8.8 284.7 %reduce-scatter.2.cloned.1.call-start = ((), (), s32[]{:S(2)}) async-start(), calls=%async_computation.2 | async-start | bytes 10027008 | tf_op jit(solution)/shard_map/reduce_scatter | solution.py:596
  31.5 17.8 %collective-permute-start.1 = (f32[384,256]{1,0:T(8,128)S(1)}, f32[384,256]{1,0:T(8,128)S(1)}, u32[]{:S(2)}, u32[]{:S(2)}) collective-permute-start(f32[384,256]{1,0:T(8,128)S(1)} %get-tuple-element.78.refs_0_), channel_id=1, source_target_pairs={{0,8},{8,16},{16,24},{1,9},{9,17},{17,25},{2,10},{10,18},{18,26},{... | collective-permute-start | bytes 1179656 | tf_op jit(solution)/shard_map/ppermute | solution.py:57
  35.8 18.7 %collective-permute-start.2 = (f32[384,256]{1,0:T(8,128)S(1)}, f32[384,256]{1,0:T(8,128)S(1)}, u32[]{:S(2)}, u32[]{:S(2)}) collective-permute-start(f32[384,256]{1,0:T(8,128)S(1)} %get-tuple-element.78.refs_0_), channel_id=1, source_target_pairs={{8,0},{16,8},{24,16},{9,1},{17,9},{25,17},{10,2},{18,10},{26,18},{... | collective-permute-start | bytes 1179656 | tf_op jit(solution)/shard_map/ppermute | solution.py:58
  54.4 24.1 %collective-permute-start.4 = (f32[384,256]{1,0:T(8,128)S(1)}, f32[384,256]{1,0:T(8,128)S(1)}, u32[]{:S(2)}, u32[]{:S(2)}) collective-permute-start(f32[384,256]{1,0:T(8,128)S(1)} %collective-permute-done.2.refs_2_), channel_id=1, source_target_pairs={{8,0},{16,8},{9,1},{17,9},{10,2},{18,10},{11,3},{19,11},{12,4},{20... | collective-permute-start | bytes 1179656 | tf_op jit(solution)/shard_map/ppermute | solution.py:58
  56.5 24.3 %collective-permute-start.5 = (f32[384,256]{1,0:T(8,128)S(1)}, f32[384,256]{1,0:T(8,128)S(1)}, u32[]{:S(2)}, u32[]{:S(2)}) collective-permute-start(f32[384,256]{1,0:T(8,128)S(1)} %collective-permute-done.3.refs_3_), channel_id=1, source_target_pairs={{16,24},{17,25},{18,26},{19,27},{20,28},{21,29},{22,30},{23,31}} | collective-permute-start | bytes 1179656 | tf_op jit(solution)/shard_map/ppermute | solution.py:57
  119.6 16.0 %collective-permute-start.7 = (f32[96,1024]{1,0:T(8,128)}, f32[96,1024]{1,0:T(8,128)S(1)}, u32[]{:S(2)}, u32[]{:S(2)}) collective-permute-start(f32[96,1024]{1,0:T(8,128)} %copy-done.88), channel_id=1, source_target_pairs={{0,8},{8,0},{16,24},{24,16},{1,9},{9,1},{17,25},{25,17},{2,10},{10... | collective-permute-start | bytes 1179656 | tf_op jit(solution)/shard_map/ppermute | solution.py:26
  135.7 18.4 %collective-permute-start.8 = (f32[96,1024]{1,0:T(8,128)}, f32[96,1024]{1,0:T(8,128)S(1)}, u32[]{:S(2)}, u32[]{:S(2)}) collective-permute-start(f32[96,1024]{1,0:T(8,128)} %copy-done.87), channel_id=1, source_target_pairs={{0,8},{8,0},{16,24},{24,16},{1,9},{9,1},{17,25},{25,17},{2,10},{10... | collective-permute-start | bytes 1179656 | tf_op jit(solution)/shard_map/ppermute | solution.py:26
  136.7 18.7 %collective-permute-start.15 = (f32[96,1024]{1,0:T(8,128)S(1)}, f32[96,1024]{1,0:T(8,128)S(1)}, u32[]{:S(2)}, u32[]{:S(2)}) collective-permute-start(f32[96,1024]{1,0:T(8,128)S(1)} %add.133), channel_id=1, source_target_pairs={{0,16},{8,24},{16,0},{24,8},{1,17},{9,25},{17,1},{25,9},{2,18},{10... | collective-permute-start | bytes 1179656 | tf_op jit(solution)/shard_map/ppermute | solution.py:26
  154.2 12.7 %collective-permute-start.17 = (f32[96,1024]{1,0:T(8,128)S(1)}, f32[96,1024]{1,0:T(8,128)S(1)}, u32[]{:S(2)}, u32[]{:S(2)}) collective-permute-start(f32[96,1024]{1,0:T(8,128)S(1)} %add.135), channel_id=1, source_target_pairs={{0,16},{8,24},{16,0},{24,8},{1,17},{9,25},{17,1},{25,9},{2,18},{10... | collective-permute-start | bytes 1179656 | tf_op jit(solution)/shard_map/ppermute | solution.py:26
  155.4 16.1 %collective-permute-start.16 = (f32[96,1024]{1,0:T(8,128)S(1)}, f32[96,1024]{1,0:T(8,128)S(1)}, u32[]{:S(2)}, u32[]{:S(2)}) collective-permute-start(f32[96,1024]{1,0:T(8,128)S(1)} %add.134.refs_0_), channel_id=1, source_target_pairs={{0,8},{8,0},{16,24},{24,16},{1,9},{9,1},{17,25},{25,17},{2,10},{10... | collective-permute-start | bytes 1179656 | tf_op jit(solution)/shard_map/ppermute | solution.py:26
  167.1 30.0 %collective-permute-start.9 = (f32[96,1024]{1,0:T(8,128)S(1)}, f32[96,1024]{1,0:T(8,128)S(1)}, u32[]{:S(2)}, u32[]{:S(2)}) collective-permute-start(f32[96,1024]{1,0:T(8,128)S(1)} %copy-done.86), channel_id=1, source_target_pairs={{0,8},{8,0},{16,24},{24,16},{1,9},{9,1},{17,25},{25,17},{2,10},{10... | collective-permute-start | bytes 1179656 | tf_op jit(solution)/shard_map/ppermute | solution.py:26
  197.1 16.8 %collective-permute-start.12 = (f32[96,1024]{1,0:T(8,128)S(1)}, f32[96,1024]{1,0:T(8,128)S(1)}, u32[]{:S(2)}, u32[]{:S(2)}) collective-permute-start(f32[96,1024]{1,0:T(8,128)S(1)} %copy-done.84), channel_id=1, source_target_pairs={{0,8},{8,0},{16,24},{24,16},{1,9},{9,1},{17,25},{25,17},{2,10},{10... | collective-permute-start | bytes 1179656 | tf_op jit(solution)/shard_map/ppermute | solution.py:26
  197.5 29.7 %collective-permute-start.10 = (f32[96,1024]{1,0:T(8,128)S(1)}, f32[96,1024]{1,0:T(8,128)S(1)}, u32[]{:S(2)}, u32[]{:S(2)}) collective-permute-start(f32[96,1024]{1,0:T(8,128)S(1)} %add.129), channel_id=1, source_target_pairs={{0,16},{8,24},{16,0},{24,8},{1,17},{9,25},{17,1},{25,9},{2,18},{10... | collective-permute-start | bytes 1179656 | tf_op jit(solution)/shard_map/ppermute | solution.py:26
  201.4 16.4 %collective-permute-start.28 = (f32[32,1024]{1,0:T(8,128)S(1)}, f32[32,1024]{1,0:T(8,128)S(1)}, u32[]{:S(2)}, u32[]{:S(2)}) collective-permute-start(f32[32,1024]{1,0:T(8,128)S(1)} %add.148), channel_id=1, source_target_pairs={{0,4},{2,6},{4,0},{6,2},{1,5},{3,7},{5,1},{7,3},{8,12},{10,14},{12... | collective-permute-start | bytes 393224 | tf_op jit(solution)/shard_map/ppermute | solution.py:26
  214.0 20.5 %collective-permute-start.13 = (f32[96,1024]{1,0:T(8,128)S(1)}, f32[96,1024]{1,0:T(8,128)S(1)}, u32[]{:S(2)}, u32[]{:S(2)}) collective-permute-start(f32[96,1024]{1,0:T(8,128)S(1)} %add.131), channel_id=1, source_target_pairs={{0,16},{8,24},{16,0},{24,8},{1,17},{9,25},{17,1},{25,9},{2,18},{10... | collective-permute-start | bytes 1179656 | tf_op jit(solution)/shard_map/ppermute | solution.py:26
  214.5 20.0 %collective-permute-start.23 = (f32[392,256]{1,0:T(8,128)S(1)}, f32[392,256]{1,0:T(8,128)S(1)}, u32[]{:S(2)}, u32[]{:S(2)}) collective-permute-start(f32[392,256]{1,0:T(8,128)S(1)} %get-tuple-element.118), channel_id=1, source_target_pairs={{24,16},{25,17},{26,18},{27,19},{28,20},{29,21},{30,22},{31,23}} | collective-permute-start | bytes 1204232 | tf_op jit(solution)/shard_map/ppermute | solution.py:822
  217.8 48.7 %collective-permute-start.31 = (f32[512,512]{1,0:T(8,128)}, f32[512,512]{1,0:T(8,128)}, u32[]{:S(2)}, u32[]{:S(2)}) collective-permute-start(f32[512,512]{1,0:T(8,128)} %get-tuple-element.123), channel_id=1, source_target_pairs={{0,1},{1,0},{2,3},{3,2},{4,5},{5,4},{6,7},{7,6},{8,9},{9,8},{10,11... | collective-permute-start | bytes 3145736 | tf_op jit(solution)/shard_map/ppermute | solution.py:26
  227.2 20.2 %collective-permute-start.11 = (f32[96,1024]{1,0:T(8,128)S(1)}, f32[96,1024]{1,0:T(8,128)}, u32[]{:S(2)}, u32[]{:S(2)}) collective-permute-start(f32[96,1024]{1,0:T(8,128)S(1)} %add.130.refs_0_), channel_id=1, source_target_pairs={{0,8},{8,0},{16,24},{24,16},{1,9},{9,1},{17,25},{25,17},{2,10},{10... | collective-permute-start | bytes 1179656 | tf_op jit(solution)/shard_map/ppermute | solution.py:26
  227.3 15.8 %collective-permute-start.20 = (f32[392,256]{1,0:T(8,128)}, f32[392,256]{1,0:T(8,128)}, u32[]{:S(2)}, u32[]{:S(2)}) collective-permute-start(f32[392,256]{1,0:T(8,128)} %get-tuple-element.115), channel_id=1, source_target_pairs={{0,8},{1,9},{2,10},{3,11},{4,12},{5,13},{6,14},{7,15}} | collective-permute-start | bytes 1204232 | tf_op jit(solution)/shard_map/ppermute | solution.py:820
  234.5 34.1 %collective-permute-start.34 = (f32[512,512]{1,0:T(8,128)}, f32[512,512]{1,0:T(8,128)}, u32[]{:S(2)}, u32[]{:S(2)}) collective-permute-start(f32[512,512]{1,0:T(8,128)} %get-tuple-element.125), channel_id=1, source_target_pairs={{0,1},{1,0},{2,3},{3,2},{4,5},{5,4},{6,7},{7,6},{8,9},{9,8},{10,11... | collective-permute-start | bytes 3145736 | tf_op jit(solution)/shard_map/ppermute | solution.py:26
  235.3 13.6 %collective-permute-start.30 = (f32[24,1024]{1,0:T(8,128)S(1)}, f32[24,1024]{1,0:T(8,128)S(1)}, u32[]{:S(2)}, u32[]{:S(2)}) collective-permute-start(f32[24,1024]{1,0:T(8,128)S(1)} %slice_add_fusion.10), channel_id=1, source_target_pairs={{0,16},{8,24},{16,0},{24,8},{1,17},{9,25},{17,1},{25,9},{2,18},{10... | collective-permute-start | bytes 294920 | tf_op jit(solution)/shard_map/ppermute | solution.py:26
  258.7 12.9 %collective-permute-start.25 = (f32[392,256]{1,0:T(8,128)S(1)}, f32[392,256]{1,0:T(8,128)S(1)}, u32[]{:S(2)}, u32[]{:S(2)}) collective-permute-start(f32[392,256]{1,0:T(8,128)S(1)} %add.143), channel_id=1, source_target_pairs={{24,16},{16,8},{8,0},{25,17},{17,9},{9,1},{26,18},{18,10},{10,2},{... | collective-permute-start | bytes 1204232 | tf_op jit(solution)/shard_map/ppermute | solution.py:822
  269.7 12.6 %collective-permute-start.35 = (f32[256,512]{1,0:T(8,128)S(1)}, f32[256,512]{1,0:T(8,128)S(1)}, u32[]{:S(2)}, u32[]{:S(2)}) collective-permute-start(f32[256,512]{1,0:T(8,128)S(1)} %slice_add_fusion), channel_id=1, source_target_pairs={{0,4},{2,6},{4,0},{6,2},{1,5},{3,7},{5,1},{7,3},{8,12},{10,14},{12... | collective-permute-start | bytes 1572872 | tf_op jit(solution)/shard_map/ppermute | solution.py:26
  (105 other events, 1079.3 us)
Sparse Core Ops, SparseCore 0:
  11.4 68.2 all-gather.1
  119.7 72.4 reduce-scatter.1
